TPU v7x, 32 devices: a whole 2x2x4 slice. The times are simulated.
32 devices in a mesh: tm: 2 (over y), space: 16 (over z, x, core).
Axes of the slice: x: 2, y: 2, z: 4, core: 2. Of those that a mesh axis runs over, the one named last changes fastest.
Arguments:
- intensity: float32 [32, 128, 512], P('tm', 'space'), may hold values from 0.05 to 5
- w_first: bfloat16 [3, 3, 48, 32], replicated, may hold values from -0.5 to 0.5
- w_rest: bfloat16 [5, 3, 3, 48, 48], replicated, may hold values from -0.4375 to 0.4375
Outputs:
- front_maps: float32 [48, 128, 512], P(None, 'space', 'tm')
All inputs are finite; a program needn't handle non-finite values.
Results may differ from a plain program's by a relative error of at most 0.03.
Values may be sent and summed in bfloat16 or wider, within the bound.
No kernel may reach another device: no remote copies, remote signals or barrier semaphores. Data moves between devices by JAX's collectives and lax.ppermute only.
A program may use at most 64 MiB of HBM per device.

v0:
```python
import jax
import jax.numpy as jnp
from jax import lax
from jax.sharding import PartitionSpec as P

LAYERS = 6
RADIUS = 3


def extended(x, sides, width):
    for axis, dim in sides:
        size, length = (lax.axis_size(axis), x.shape[dim])
        up = [(i, (i + 1) % size) for i in range(size - 1)]
        down = [(j, i) for i, j in up]
        last = lax.slice_in_dim(x, length - width, length, axis=dim)
        leading = lax.slice_in_dim(x, 0, width, axis=dim)
        before = lax.ppermute(last, axis, up)
        after = lax.ppermute(leading, axis, down)
        x = jnp.concatenate([before, x, after], axis=dim)
    return x


def window_count(start_place, length, overall):
    places = start_place + jnp.arange(length, dtype=jnp.int32)
    upper = jnp.minimum(places + RADIUS, overall - 1)
    lower = jnp.maximum(places - RADIUS, 0)
    return (upper - lower + 1).astype(jnp.float32)


def conv_tile(padded, kernel):
    out_cols = padded.shape[1] - 2
    out_rows = padded.shape[2] - 2
    summed = None
    for a in range(3):
        for b in range(3):
            product = jnp.einsum(
                "oi,ixy->oxy",
                kernel[a, b],
                padded[:, a : a + out_cols, b : b + out_rows],
                preferred_element_type=jnp.float32,
            )
            summed = product if summed is None else summed + product
    return summed


def shards(intensity, w_first, w_rest):
    acq_dev, col_span, row_span = intensity.shape
    space_count = lax.axis_size("space")
    tm_count = lax.axis_size("tm")
    col_start = lax.axis_index("space") * col_span
    widened = extended(intensity, (("space", 1),), RADIUS)
    col_sum = widened[:, 0:col_span, :]
    for k in range(1, 2 * RADIUS + 1):
        col_sum = col_sum + widened[:, k : k + col_span, :]
    row_padded = jnp.pad(col_sum, ((0, 0), (0, 0), (RADIUS, RADIUS)))
    box_sum = row_padded[:, :, 0:row_span]
    for k in range(1, 2 * RADIUS + 1):
        box_sum = box_sum + row_padded[:, :, k : k + row_span]
    cell_count = (
        window_count(col_start, col_span, col_span * space_count)[:, None]
        * window_count(0, row_span, row_span)[None, :]
    )
    local_mean = box_sum / cell_count
    log_mean = jnp.log(local_mean)
    ratio_part = jnp.sum(intensity / local_mean, axis=0)
    acq_total = acq_dev * tm_count
    ratio_sum = lax.psum(ratio_part, "tm")
    features_own = (log_mean + jnp.log(ratio_sum / acq_total)[None]).astype(jnp.bfloat16)
    features = lax.all_to_all(features_own, "tm", split_axis=2, concat_axis=0, tiled=True)
    kernels = [w_first] + [w_rest[k] for k in range(LAYERS - 1)]
    activation = features
    result = None
    for depth_index in range(LAYERS):
        padded = extended(activation, (("tm", 2), ("space", 1)), 1)
        summed = conv_tile(padded, kernels[depth_index])
        if depth_index < LAYERS - 1:
            activation = jnp.maximum(summed, 0.0).astype(jnp.bfloat16)
        else:
            result = summed
    return result


def solution(mesh):
    in_specs = (P("tm", "space", None), P(), P())
    out_specs = P(None, "space", "tm")
    return jax.shard_map(shards, mesh=mesh, in_specs=in_specs, out_specs=out_specs, check_vma=False)
```

profile of v0, /device:TPU:19, one launch (start us, length us, event | category | flops | bytes accessed | tf_op | source)
XLA Modules:
  0.0 145.4 jit_solution(1917381582807719595)
XLA Ops:
  0.0 1.1 fusion.193
  1.1 2.7 %collective-permute-start.1 = (f32[16,3,512]{2,0,1:T(8,128)S(1)}, f32[16,3,512]{2,0,1:T(8,128)S(1)}, u32[]{:S(2)}, u32[]{:S(2)}) collective-permute-start(f32[16,3,512]{2,0,1:T(8,128)S(1)} %copy.56), channel_id=1, source_target_pairs={{1,0},{2,1},{3,2},{4,3},{5,4},{6,5},{7,6},{8,7},{9,8},{10,9},{11,1... | collective-permute-start | bytes 294920 | tf_op jit(solution)/shard_map/ppermute | solution.py:18
  3.9 3.9 %collective-permute-start = (f32[16,3,512]{2,0,1:T(8,128)S(1)}, f32[16,3,512]{2,0,1:T(8,128)S(1)}, u32[]{:S(2)}, u32[]{:S(2)}) collective-permute-start(f32[16,3,512]{2,0,1:T(8,128)S(1)} %copy.55), channel_id=1, source_target_pairs={{0,1},{1,2},{2,3},{3,4},{4,5},{5,6},{6,7},{7,8},{8,9},{9,10},{10,1... | collective-permute-start | bytes 294920 | tf_op jit(solution)/shard_map/ppermute | solution.py:17
  7.9 1.5 %collective-permute-done = f32[16,3,512]{2,0,1:T(8,128)S(1)} collective-permute-done((f32[16,3,512]{2,0,1:T(8,128)S(1)}, f32[16,3,512]{2,0,1:T(8,128)S(1)}, u32[]{:S(2)}, u32[]{:S(2)}) %collective-permute-start) | collective-permute-done | bytes 98336 | tf_op jit(solution)/shard_map/ppermute | solution.py:17
  9.8 0.5 fusion.66
  10.3 6.2 %psum.7 = f32[8,512]{1,0:T(8,128)S(1)} all-reduce(f32[8,512]{1,0:T(8,128)S(1)} %get-tuple-element.5), channel_id=1, replica_groups=mesh['tm'=2,'space'=16] {'tm'}, use_global_device_ids=true, to_apply=%region_1.2 | all-reduce | flops 4096 | bytes 32768 | tf_op jit(solution)/shard_map/psum | solution.py:67
  16.6 0.8 copy.52
  17.4 1.7 %reshape.104 = bf16[2,2,16384]{2,1,0:T(2,128)(2,1)} reshape(bf16[512,8,16]{2,1,0:T(8,128)(2,1)S(1)} %bitcast.310) | data formatting | bytes 262144
  19.1 3.4 %all-to-all-start = ((bf16[2,2,16384]{2,1,0:T(2,128)(2,1)}), bf16[2,2,16384]{2,1,0:T(2,128)(2,1)S(1)}, u32[]{:S(2)}, u32[]{:S(2)}) async-start(bf16[2,2,16384]{2,1,0:T(2,128)(2,1)} %reshape.104), calls=%async_computation | async-start | bytes 262144 | tf_op jit(solution)/shard_map/all_to_all | solution.py:69
  22.6 3.3 %all-to-all-done = bf16[2,2,16384]{2,1,0:T(2,128)(2,1)S(1)} async-done(((bf16[2,2,16384]{2,1,0:T(2,128)(2,1)}), bf16[2,2,16384]{2,1,0:T(2,128)(2,1)S(1)}, u32[]{:S(2)}, u32[]{:S(2)}) %all-to-all-start) | async-done | bytes 131104 | tf_op jit(solution)/shard_map/all_to_all | solution.py:69
  25.8 0.7 reshape.105
  26.5 0.7 copy.53
  27.3 1.9 %collective-permute-start.2 = (bf16[32,8,1]{2,0,1:T(8,128)(2,1)S(1)}, bf16[32,8,1]{2,0,1:T(8,128)(2,1)S(1)}, u32[]{:S(2)}, u32[]{:S(2)}) collective-permute-start(bf16[32,8,1]{2,0,1:T(8,128)(2,1)S(1)} %get-tuple-element.48), channel_id=1, source_target_pairs={{0,16},{1,17},{2,18},{3,19},{4,20},{5,21},{6,22},{7,23},{8,24},{9,... | collective-permute-start | bytes 1544 | tf_op jit(solution)/shard_map/ppermute | solution.py:17
  29.2 1.3 collective-permute-start.3
  30.8 3.4 %collective-permute-done.3 = bf16[32,8,1]{2,0,1:T(8,128)(2,1)S(1)} collective-permute-done((bf16[32,8,1]{2,0,1:T(8,128)(2,1)S(1)}, bf16[32,8,1]{2,0,1:T(8,128)(2,1)S(1)}, u32[]{:S(2)}, u32[]{:S(2)}) %collective-permute-start.3) | collective-permute-done | bytes 544 | tf_op jit(solution)/shard_map/ppermute | solution.py:18
  34.4 9.5 %collective-permute-start.4 = (bf16[32,1,258]{2,0,1:T(8,128)(2,1)S(1)}, bf16[32,1,258]{2,0,1:T(8,128)(2,1)S(1)}, u32[]{:S(2)}, u32[]{:S(2)}) collective-permute-start(bf16[32,1,258]{2,0,1:T(8,128)(2,1)S(1)} %get-tuple-element.34), channel_id=1, source_target_pairs={{0,1},{1,2},{2,3},{3,4},{4,5},{5,6},{6,7},{7,8},{8,9},{9,10},{10,1... | collective-permute-start | bytes 49544 | tf_op jit(solution)/shard_map/ppermute | solution.py:17
  43.9 1.9 %collective-permute-start.5 = (bf16[32,1,258]{2,0,1:T(8,128)(2,1)S(1)}, bf16[32,1,258]{2,0,1:T(8,128)(2,1)S(1)}, u32[]{:S(2)}, u32[]{:S(2)}) collective-permute-start(bf16[32,1,258]{2,0,1:T(8,128)(2,1)S(1)} %get-tuple-element.35), channel_id=1, source_target_pairs={{1,0},{2,1},{3,2},{4,3},{5,4},{6,5},{7,6},{8,7},{9,8},{10,9},{11,1... | collective-permute-start | bytes 49544 | tf_op jit(solution)/shard_map/ppermute | solution.py:18
  46.1 3.8 %collective-permute-done.5 = bf16[32,1,258]{2,0,1:T(8,128)(2,1)S(1)} collective-permute-done((bf16[32,1,258]{2,0,1:T(8,128)(2,1)S(1)}, bf16[32,1,258]{2,0,1:T(8,128)(2,1)S(1)}, u32[]{:S(2)}, u32[]{:S(2)}) %collective-permute-start.5) | collective-permute-done | bytes 16544 | tf_op jit(solution)/shard_map/ppermute | solution.py:18
  50.4 0.3 fusion.148
  50.7 0.3 fusion.137
  51.0 0.3 fusion.139
  51.5 0.3 fusion.41
  51.8 0.3 fusion.51
  52.3 1.3 collective-permute-start.6
  53.6 1.3 collective-permute-start.7
  55.2 3.7 %collective-permute-done.7 = bf16[48,8,1]{2,0,1:T(8,128)(2,1)S(1)} collective-permute-done((bf16[48,8,1]{2,0,1:T(8,128)(2,1)S(1)}, bf16[48,8,1]{2,0,1:T(8,128)(2,1)S(1)}, u32[]{:S(2)}, u32[]{:S(2)}) %collective-permute-start.7) | collective-permute-done | bytes 800 | tf_op jit(solution)/shard_map/ppermute | solution.py:18
  59.0 3.4 %collective-permute-start.8 = (bf16[48,1,258]{2,0,1:T(8,128)(2,1)S(1)}, bf16[48,1,258]{2,0,1:T(8,128)(2,1)S(1)}, u32[]{:S(2)}, u32[]{:S(2)}) collective-permute-start(bf16[48,1,258]{2,0,1:T(8,128)(2,1)S(1)} %get-tuple-element.30), channel_id=1, source_target_pairs={{0,1},{1,2},{2,3},{3,4},{4,5},{5,6},{6,7},{7,8},{8,9},{9,10},{10,1... | collective-permute-start | bytes 74312 | tf_op jit(solution)/shard_map/ppermute | solution.py:17
  62.4 1.9 %collective-permute-start.9 = (bf16[48,1,258]{2,0,1:T(8,128)(2,1)S(1)}, bf16[48,1,258]{2,0,1:T(8,128)(2,1)S(1)}, u32[]{:S(2)}, u32[]{:S(2)}) collective-permute-start(bf16[48,1,258]{2,0,1:T(8,128)(2,1)S(1)} %get-tuple-element.31), channel_id=1, source_target_pairs={{1,0},{2,1},{3,2},{4,3},{5,4},{6,5},{7,6},{8,7},{9,8},{10,9},{11,1... | collective-permute-start | bytes 74312 | tf_op jit(solution)/shard_map/ppermute | solution.py:18
  64.6 4.0 %collective-permute-done.9 = bf16[48,1,258]{2,0,1:T(8,128)(2,1)S(1)} collective-permute-done((bf16[48,1,258]{2,0,1:T(8,128)(2,1)S(1)}, bf16[48,1,258]{2,0,1:T(8,128)(2,1)S(1)}, u32[]{:S(2)}, u32[]{:S(2)}) %collective-permute-start.9) | collective-permute-done | bytes 24800 | tf_op jit(solution)/shard_map/ppermute | solution.py:18
  68.6 0.3 maximum_maximum_fusion
  70.3 0.3 fusion.50
  70.8 1.3 collective-permute-start.10
  72.1 1.3 collective-permute-start.11
  73.7 3.7 %collective-permute-done.11 = bf16[48,8,1]{2,0,1:T(8,128)(2,1)S(1)} collective-permute-done((bf16[48,8,1]{2,0,1:T(8,128)(2,1)S(1)}, bf16[48,8,1]{2,0,1:T(8,128)(2,1)S(1)}, u32[]{:S(2)}, u32[]{:S(2)}) %collective-permute-start.11) | collective-permute-done | bytes 800 | tf_op jit(solution)/shard_map/ppermute | solution.py:18
  77.5 3.3 %collective-permute-start.12 = (bf16[48,1,258]{2,0,1:T(8,128)(2,1)S(1)}, bf16[48,1,258]{2,0,1:T(8,128)(2,1)S(1)}, u32[]{:S(2)}, u32[]{:S(2)}) collective-permute-start(bf16[48,1,258]{2,0,1:T(8,128)(2,1)S(1)} %get-tuple-element.26), channel_id=1, source_target_pairs={{0,1},{1,2},{2,3},{3,4},{4,5},{5,6},{6,7},{7,8},{8,9},{9,10},{10,1... | collective-permute-start | bytes 74312 | tf_op jit(solution)/shard_map/ppermute | solution.py:17
  80.8 1.9 %collective-permute-start.13 = (bf16[48,1,258]{2,0,1:T(8,128)(2,1)S(1)}, bf16[48,1,258]{2,0,1:T(8,128)(2,1)S(1)}, u32[]{:S(2)}, u32[]{:S(2)}) collective-permute-start(bf16[48,1,258]{2,0,1:T(8,128)(2,1)S(1)} %get-tuple-element.27), channel_id=1, source_target_pairs={{1,0},{2,1},{3,2},{4,3},{5,4},{6,5},{7,6},{8,7},{9,8},{10,9},{11,1... | collective-permute-start | bytes 74312 | tf_op jit(solution)/shard_map/ppermute | solution.py:18
  83.0 4.0 %collective-permute-done.13 = bf16[48,1,258]{2,0,1:T(8,128)(2,1)S(1)} collective-permute-done((bf16[48,1,258]{2,0,1:T(8,128)(2,1)S(1)}, bf16[48,1,258]{2,0,1:T(8,128)(2,1)S(1)}, u32[]{:S(2)}, u32[]{:S(2)}) %collective-permute-start.13) | collective-permute-done | bytes 24800 | tf_op jit(solution)/shard_map/ppermute | solution.py:18
  87.0 0.3 maximum_maximum_fusion.1
  88.8 0.3 fusion.49
  89.2 1.3 collective-permute-start.14
  90.5 1.3 collective-permute-start.15
  92.1 3.7 %collective-permute-done.15 = bf16[48,8,1]{2,0,1:T(8,128)(2,1)S(1)} collective-permute-done((bf16[48,8,1]{2,0,1:T(8,128)(2,1)S(1)}, bf16[48,8,1]{2,0,1:T(8,128)(2,1)S(1)}, u32[]{:S(2)}, u32[]{:S(2)}) %collective-permute-start.15) | collective-permute-done | bytes 800 | tf_op jit(solution)/shard_map/ppermute | solution.py:18
  96.0 3.3 %collective-permute-start.16 = (bf16[48,1,258]{2,0,1:T(8,128)(2,1)S(1)}, bf16[48,1,258]{2,0,1:T(8,128)(2,1)S(1)}, u32[]{:S(2)}, u32[]{:S(2)}) collective-permute-start(bf16[48,1,258]{2,0,1:T(8,128)(2,1)S(1)} %get-tuple-element.22), channel_id=1, source_target_pairs={{0,1},{1,2},{2,3},{3,4},{4,5},{5,6},{6,7},{7,8},{8,9},{9,10},{10,1... | collective-permute-start | bytes 74312 | tf_op jit(solution)/shard_map/ppermute | solution.py:17
  99.3 2.1 %collective-permute-start.17 = (bf16[48,1,258]{2,0,1:T(8,128)(2,1)S(1)}, bf16[48,1,258]{2,0,1:T(8,128)(2,1)S(1)}, u32[]{:S(2)}, u32[]{:S(2)}) collective-permute-start(bf16[48,1,258]{2,0,1:T(8,128)(2,1)S(1)} %get-tuple-element.23), channel_id=1, source_target_pairs={{1,0},{2,1},{3,2},{4,3},{5,4},{6,5},{7,6},{8,7},{9,8},{10,9},{11,1... | collective-permute-start | bytes 74312 | tf_op jit(solution)/shard_map/ppermute | solution.py:18
  101.7 3.8 %collective-permute-done.17 = bf16[48,1,258]{2,0,1:T(8,128)(2,1)S(1)} collective-permute-done((bf16[48,1,258]{2,0,1:T(8,128)(2,1)S(1)}, bf16[48,1,258]{2,0,1:T(8,128)(2,1)S(1)}, u32[]{:S(2)}, u32[]{:S(2)}) %collective-permute-start.17) | collective-permute-done | bytes 24800 | tf_op jit(solution)/shard_map/ppermute | solution.py:18
  105.5 0.3 maximum_maximum_fusion.2
  107.2 0.3 fusion.48
  107.6 1.3 collective-permute-start.18
  109.0 1.3 collective-permute-start.19
  110.6 3.7 %collective-permute-done.19 = bf16[48,8,1]{2,0,1:T(8,128)(2,1)S(1)} collective-permute-done((bf16[48,8,1]{2,0,1:T(8,128)(2,1)S(1)}, bf16[48,8,1]{2,0,1:T(8,128)(2,1)S(1)}, u32[]{:S(2)}, u32[]{:S(2)}) %collective-permute-start.19) | collective-permute-done | bytes 800 | tf_op jit(solution)/shard_map/ppermute | solution.py:18
  114.4 3.3 %collective-permute-start.20 = (bf16[48,1,258]{2,0,1:T(8,128)(2,1)S(1)}, bf16[48,1,258]{2,0,1:T(8,128)(2,1)S(1)}, u32[]{:S(2)}, u32[]{:S(2)}) collective-permute-start(bf16[48,1,258]{2,0,1:T(8,128)(2,1)S(1)} %get-tuple-element.18), channel_id=1, source_target_pairs={{0,1},{1,2},{2,3},{3,4},{4,5},{5,6},{6,7},{7,8},{8,9},{9,10},{10,1... | collective-permute-start | bytes 74312 | tf_op jit(solution)/shard_map/ppermute | solution.py:17
  117.7 1.9 %collective-permute-start.21 = (bf16[48,1,258]{2,0,1:T(8,128)(2,1)S(1)}, bf16[48,1,258]{2,0,1:T(8,128)(2,1)S(1)}, u32[]{:S(2)}, u32[]{:S(2)}) collective-permute-start(bf16[48,1,258]{2,0,1:T(8,128)(2,1)S(1)} %get-tuple-element.19), channel_id=1, source_target_pairs={{1,0},{2,1},{3,2},{4,3},{5,4},{6,5},{7,6},{8,7},{9,8},{10,9},{11,1... | collective-permute-start | bytes 74312 | tf_op jit(solution)/shard_map/ppermute | solution.py:18
  119.9 4.0 %collective-permute-done.21 = bf16[48,1,258]{2,0,1:T(8,128)(2,1)S(1)} collective-permute-done((bf16[48,1,258]{2,0,1:T(8,128)(2,1)S(1)}, bf16[48,1,258]{2,0,1:T(8,128)(2,1)S(1)}, u32[]{:S(2)}, u32[]{:S(2)}) %collective-permute-start.21) | collective-permute-done | bytes 24800 | tf_op jit(solution)/shard_map/ppermute | solution.py:18
  123.9 0.3 maximum_maximum_fusion.3
  125.7 0.3 fusion.47
  126.1 1.3 collective-permute-start.22
  127.4 1.3 collective-permute-start.23
  129.0 3.7 %collective-permute-done.23 = bf16[48,8,1]{2,0,1:T(8,128)(2,1)S(1)} collective-permute-done((bf16[48,8,1]{2,0,1:T(8,128)(2,1)S(1)}, bf16[48,8,1]{2,0,1:T(8,128)(2,1)S(1)}, u32[]{:S(2)}, u32[]{:S(2)}) %collective-permute-start.23) | collective-permute-done | bytes 800 | tf_op jit(solution)/shard_map/ppermute | solution.py:18
  132.8 3.3 %collective-permute-start.24 = (bf16[48,1,258]{2,0,1:T(8,128)(2,1)S(1)}, bf16[48,1,258]{2,0,1:T(8,128)(2,1)S(1)}, u32[]{:S(2)}, u32[]{:S(2)}) collective-permute-start(bf16[48,1,258]{2,0,1:T(8,128)(2,1)S(1)} %get-tuple-element.14), channel_id=1, source_target_pairs={{0,1},{1,2},{2,3},{3,4},{4,5},{5,6},{6,7},{7,8},{8,9},{9,10},{10,1... | collective-permute-start | bytes 74312 | tf_op jit(solution)/shard_map/ppermute | solution.py:17
  136.1 1.9 %collective-permute-start.25 = (bf16[48,1,258]{2,0,1:T(8,128)(2,1)S(1)}, bf16[48,1,258]{2,0,1:T(8,128)(2,1)S(1)}, u32[]{:S(2)}, u32[]{:S(2)}) collective-permute-start(bf16[48,1,258]{2,0,1:T(8,128)(2,1)S(1)} %get-tuple-element.15), channel_id=1, source_target_pairs={{1,0},{2,1},{3,2},{4,3},{5,4},{6,5},{7,6},{8,7},{9,8},{10,9},{11,1... | collective-permute-start | bytes 74312 | tf_op jit(solution)/shard_map/ppermute | solution.py:18
  138.3 4.0 %collective-permute-done.25 = bf16[48,1,258]{2,0,1:T(8,128)(2,1)S(1)} collective-permute-done((bf16[48,1,258]{2,0,1:T(8,128)(2,1)S(1)}, bf16[48,1,258]{2,0,1:T(8,128)(2,1)S(1)}, u32[]{:S(2)}, u32[]{:S(2)}) %collective-permute-start.25) | collective-permute-done | bytes 24800 | tf_op jit(solution)/shard_map/ppermute | solution.py:18
  142.3 0.3 maximum_maximum_fusion.4
  144.1 0.3 fusion.14
  144.4 1.0 copy.54
  (88 shorter events, 13.2 us)
Async XLA Ops:
  1.1 6.8 %copy-start = (f32[16,8,512]{2,1,0:T(8,128)S(1)}, f32[16,8,512]{2,1,0:T(8,128)}, u32[]{:S(2)}) copy-start(f32[16,8,512]{2,1,0:T(8,128)} %param.3) | copy-start | bytes 786436
  1.1 8.3 %collective-permute-start.1 = (f32[16,3,512]{2,0,1:T(8,128)S(1)}, f32[16,3,512]{2,0,1:T(8,128)S(1)}, u32[]{:S(2)}, u32[]{:S(2)}) collective-permute-start(f32[16,3,512]{2,0,1:T(8,128)S(1)} %copy.56), channel_id=1, source_target_pairs={{1,0},{2,1},{3,2},{4,3},{5,4},{6,5},{7,6},{8,7},{9,8},{10,9},{11,1... | collective-permute-start | bytes 294920 | tf_op jit(solution)/shard_map/ppermute | solution.py:18
  3.9 5.5 %collective-permute-start = (f32[16,3,512]{2,0,1:T(8,128)S(1)}, f32[16,3,512]{2,0,1:T(8,128)S(1)}, u32[]{:S(2)}, u32[]{:S(2)}) collective-permute-start(f32[16,3,512]{2,0,1:T(8,128)S(1)} %copy.55), channel_id=1, source_target_pairs={{0,1},{1,2},{2,3},{3,4},{4,5},{5,6},{6,7},{7,8},{8,9},{9,10},{10,1... | collective-permute-start | bytes 294920 | tf_op jit(solution)/shard_map/ppermute | solution.py:17
  17.4 5.1 %copy-start.1 = (bf16[5,3,3,48,48]{4,3,2,1,0:T(8,128)(2,1)S(1)}, bf16[5,3,3,48,48]{4,3,2,1,0:T(8,128)(2,1)}, u32[]{:S(2)}) copy-start(bf16[5,3,3,48,48]{4,3,2,1,0:T(8,128)(2,1)} %param.5) | copy-start | bytes 622084
  19.1 6.7 %all-to-all-start = ((bf16[2,2,16384]{2,1,0:T(2,128)(2,1)}), bf16[2,2,16384]{2,1,0:T(2,128)(2,1)S(1)}, u32[]{:S(2)}, u32[]{:S(2)}) async-start(bf16[2,2,16384]{2,1,0:T(2,128)(2,1)} %reshape.104), calls=%async_computation | async-start | bytes 262144 | tf_op jit(solution)/shard_map/all_to_all | solution.py:69
  27.2 3.3 %copy-start.2 = (bf16[3,3,48,32]{2,3,1,0:T(8,128)(2,1)S(1)}, bf16[3,3,48,32]{2,3,1,0:T(8,128)(2,1)}, u32[]{:S(2)}) copy-start(bf16[3,3,48,32]{2,3,1,0:T(8,128)(2,1)} %param.4) | copy-start | bytes 82948
  27.3 3.5 %collective-permute-start.2 = (bf16[32,8,1]{2,0,1:T(8,128)(2,1)S(1)}, bf16[32,8,1]{2,0,1:T(8,128)(2,1)S(1)}, u32[]{:S(2)}, u32[]{:S(2)}) collective-permute-start(bf16[32,8,1]{2,0,1:T(8,128)(2,1)S(1)} %get-tuple-element.48), channel_id=1, source_target_pairs={{0,16},{1,17},{2,18},{3,19},{4,20},{5,21},{6,22},{7,23},{8,24},{9,... | collective-permute-start | bytes 1544 | tf_op jit(solution)/shard_map/ppermute | solution.py:17
  29.2 5.0 %collective-permute-start.3 = (bf16[32,8,1]{2,0,1:T(8,128)(2,1)S(1)}, bf16[32,8,1]{2,0,1:T(8,128)(2,1)S(1)}, u32[]{:S(2)}, u32[]{:S(2)}) collective-permute-start(bf16[32,8,1]{2,0,1:T(8,128)(2,1)S(1)} %get-tuple-element.49), channel_id=1, source_target_pairs={{16,0},{17,1},{18,2},{19,3},{20,4},{21,5},{22,6},{23,7},{24,8},{25... | collective-permute-start | bytes 1544 | tf_op jit(solution)/shard_map/ppermute | solution.py:18
  34.4 11.8 %collective-permute-start.4 = (bf16[32,1,258]{2,0,1:T(8,128)(2,1)S(1)}, bf16[32,1,258]{2,0,1:T(8,128)(2,1)S(1)}, u32[]{:S(2)}, u32[]{:S(2)}) collective-permute-start(bf16[32,1,258]{2,0,1:T(8,128)(2,1)S(1)} %get-tuple-element.34), channel_id=1, source_target_pairs={{0,1},{1,2},{2,3},{3,4},{4,5},{5,6},{6,7},{7,8},{8,9},{9,10},{10,1... | collective-permute-start | bytes 49544 | tf_op jit(solution)/shard_map/ppermute | solution.py:17
  43.9 6.0 %collective-permute-start.5 = (bf16[32,1,258]{2,0,1:T(8,128)(2,1)S(1)}, bf16[32,1,258]{2,0,1:T(8,128)(2,1)S(1)}, u32[]{:S(2)}, u32[]{:S(2)}) collective-permute-start(bf16[32,1,258]{2,0,1:T(8,128)(2,1)S(1)} %get-tuple-element.35), channel_id=1, source_target_pairs={{1,0},{2,1},{3,2},{4,3},{5,4},{6,5},{7,6},{8,7},{9,8},{10,9},{11,1... | collective-permute-start | bytes 49544 | tf_op jit(solution)/shard_map/ppermute | solution.py:18
  52.3 2.9 %collective-permute-start.6 = (bf16[48,8,1]{2,0,1:T(8,128)(2,1)S(1)}, bf16[48,8,1]{2,0,1:T(8,128)(2,1)S(1)}, u32[]{:S(2)}, u32[]{:S(2)}) collective-permute-start(bf16[48,8,1]{2,0,1:T(8,128)(2,1)S(1)} %get-tuple-element.46), channel_id=1, source_target_pairs={{0,16},{1,17},{2,18},{3,19},{4,20},{5,21},{6,22},{7,23},{8,24},{9,... | collective-permute-start | bytes 2312 | tf_op jit(solution)/shard_map/ppermute | solution.py:17
  53.6 5.4 %collective-permute-start.7 = (bf16[48,8,1]{2,0,1:T(8,128)(2,1)S(1)}, bf16[48,8,1]{2,0,1:T(8,128)(2,1)S(1)}, u32[]{:S(2)}, u32[]{:S(2)}) collective-permute-start(bf16[48,8,1]{2,0,1:T(8,128)(2,1)S(1)} %get-tuple-element.47), channel_id=1, source_target_pairs={{16,0},{17,1},{18,2},{19,3},{20,4},{21,5},{22,6},{23,7},{24,8},{25... | collective-permute-start | bytes 2312 | tf_op jit(solution)/shard_map/ppermute | solution.py:18
  59.0 5.6 %collective-permute-start.8 = (bf16[48,1,258]{2,0,1:T(8,128)(2,1)S(1)}, bf16[48,1,258]{2,0,1:T(8,128)(2,1)S(1)}, u32[]{:S(2)}, u32[]{:S(2)}) collective-permute-start(bf16[48,1,258]{2,0,1:T(8,128)(2,1)S(1)} %get-tuple-element.30), channel_id=1, source_target_pairs={{0,1},{1,2},{2,3},{3,4},{4,5},{5,6},{6,7},{7,8},{8,9},{9,10},{10,1... | collective-permute-start | bytes 74312 | tf_op jit(solution)/shard_map/ppermute | solution.py:17
  62.4 6.2 %collective-permute-start.9 = (bf16[48,1,258]{2,0,1:T(8,128)(2,1)S(1)}, bf16[48,1,258]{2,0,1:T(8,128)(2,1)S(1)}, u32[]{:S(2)}, u32[]{:S(2)}) collective-permute-start(bf16[48,1,258]{2,0,1:T(8,128)(2,1)S(1)} %get-tuple-element.31), channel_id=1, source_target_pairs={{1,0},{2,1},{3,2},{4,3},{5,4},{6,5},{7,6},{8,7},{9,8},{10,9},{11,1... | collective-permute-start | bytes 74312 | tf_op jit(solution)/shard_map/ppermute | solution.py:18
  70.8 2.9 %collective-permute-start.10 = (bf16[48,8,1]{2,0,1:T(8,128)(2,1)S(1)}, bf16[48,8,1]{2,0,1:T(8,128)(2,1)S(1)}, u32[]{:S(2)}, u32[]{:S(2)}) collective-permute-start(bf16[48,8,1]{2,0,1:T(8,128)(2,1)S(1)} %get-tuple-element.44), channel_id=1, source_target_pairs={{0,16},{1,17},{2,18},{3,19},{4,20},{5,21},{6,22},{7,23},{8,24},{9,... | collective-permute-start | bytes 2312 | tf_op jit(solution)/shard_map/ppermute | solution.py:17
  72.1 5.4 %collective-permute-start.11 = (bf16[48,8,1]{2,0,1:T(8,128)(2,1)S(1)}, bf16[48,8,1]{2,0,1:T(8,128)(2,1)S(1)}, u32[]{:S(2)}, u32[]{:S(2)}) collective-permute-start(bf16[48,8,1]{2,0,1:T(8,128)(2,1)S(1)} %get-tuple-element.45), channel_id=1, source_target_pairs={{16,0},{17,1},{18,2},{19,3},{20,4},{21,5},{22,6},{23,7},{24,8},{25... | collective-permute-start | bytes 2312 | tf_op jit(solution)/shard_map/ppermute | solution.py:18
  77.5 5.5 %collective-permute-start.12 = (bf16[48,1,258]{2,0,1:T(8,128)(2,1)S(1)}, bf16[48,1,258]{2,0,1:T(8,128)(2,1)S(1)}, u32[]{:S(2)}, u32[]{:S(2)}) collective-permute-start(bf16[48,1,258]{2,0,1:T(8,128)(2,1)S(1)} %get-tuple-element.26), channel_id=1, source_target_pairs={{0,1},{1,2},{2,3},{3,4},{4,5},{5,6},{6,7},{7,8},{8,9},{9,10},{10,1... | collective-permute-start | bytes 74312 | tf_op jit(solution)/shard_map/ppermute | solution.py:17
  80.8 6.2 %collective-permute-start.13 = (bf16[48,1,258]{2,0,1:T(8,128)(2,1)S(1)}, bf16[48,1,258]{2,0,1:T(8,128)(2,1)S(1)}, u32[]{:S(2)}, u32[]{:S(2)}) collective-permute-start(bf16[48,1,258]{2,0,1:T(8,128)(2,1)S(1)} %get-tuple-element.27), channel_id=1, source_target_pairs={{1,0},{2,1},{3,2},{4,3},{5,4},{6,5},{7,6},{8,7},{9,8},{10,9},{11,1... | collective-permute-start | bytes 74312 | tf_op jit(solution)/shard_map/ppermute | solution.py:18
  89.2 2.9 %collective-permute-start.14 = (bf16[48,8,1]{2,0,1:T(8,128)(2,1)S(1)}, bf16[48,8,1]{2,0,1:T(8,128)(2,1)S(1)}, u32[]{:S(2)}, u32[]{:S(2)}) collective-permute-start(bf16[48,8,1]{2,0,1:T(8,128)(2,1)S(1)} %get-tuple-element.42), channel_id=1, source_target_pairs={{0,16},{1,17},{2,18},{3,19},{4,20},{5,21},{6,22},{7,23},{8,24},{9,... | collective-permute-start | bytes 2312 | tf_op jit(solution)/shard_map/ppermute | solution.py:17
  90.5 5.4 %collective-permute-start.15 = (bf16[48,8,1]{2,0,1:T(8,128)(2,1)S(1)}, bf16[48,8,1]{2,0,1:T(8,128)(2,1)S(1)}, u32[]{:S(2)}, u32[]{:S(2)}) collective-permute-start(bf16[48,8,1]{2,0,1:T(8,128)(2,1)S(1)} %get-tuple-element.43), channel_id=1, source_target_pairs={{16,0},{17,1},{18,2},{19,3},{20,4},{21,5},{22,6},{23,7},{24,8},{25... | collective-permute-start | bytes 2312 | tf_op jit(solution)/shard_map/ppermute | solution.py:18
  96.0 5.7 %collective-permute-start.16 = (bf16[48,1,258]{2,0,1:T(8,128)(2,1)S(1)}, bf16[48,1,258]{2,0,1:T(8,128)(2,1)S(1)}, u32[]{:S(2)}, u32[]{:S(2)}) collective-permute-start(bf16[48,1,258]{2,0,1:T(8,128)(2,1)S(1)} %get-tuple-element.22), channel_id=1, source_target_pairs={{0,1},{1,2},{2,3},{3,4},{4,5},{5,6},{6,7},{7,8},{8,9},{9,10},{10,1... | collective-permute-start | bytes 74312 | tf_op jit(solution)/shard_map/ppermute | solution.py:17
  99.3 6.2 %collective-permute-start.17 = (bf16[48,1,258]{2,0,1:T(8,128)(2,1)S(1)}, bf16[48,1,258]{2,0,1:T(8,128)(2,1)S(1)}, u32[]{:S(2)}, u32[]{:S(2)}) collective-permute-start(bf16[48,1,258]{2,0,1:T(8,128)(2,1)S(1)} %get-tuple-element.23), channel_id=1, source_target_pairs={{1,0},{2,1},{3,2},{4,3},{5,4},{6,5},{7,6},{8,7},{9,8},{10,9},{11,1... | collective-permute-start | bytes 74312 | tf_op jit(solution)/shard_map/ppermute | solution.py:18
  107.6 2.9 %collective-permute-start.18 = (bf16[48,8,1]{2,0,1:T(8,128)(2,1)S(1)}, bf16[48,8,1]{2,0,1:T(8,128)(2,1)S(1)}, u32[]{:S(2)}, u32[]{:S(2)}) collective-permute-start(bf16[48,8,1]{2,0,1:T(8,128)(2,1)S(1)} %get-tuple-element.40), channel_id=1, source_target_pairs={{0,16},{1,17},{2,18},{3,19},{4,20},{5,21},{6,22},{7,23},{8,24},{9,... | collective-permute-start | bytes 2312 | tf_op jit(solution)/shard_map/ppermute | solution.py:17
  109.0 5.4 %collective-permute-start.19 = (bf16[48,8,1]{2,0,1:T(8,128)(2,1)S(1)}, bf16[48,8,1]{2,0,1:T(8,128)(2,1)S(1)}, u32[]{:S(2)}, u32[]{:S(2)}) collective-permute-start(bf16[48,8,1]{2,0,1:T(8,128)(2,1)S(1)} %get-tuple-element.41), channel_id=1, source_target_pairs={{16,0},{17,1},{18,2},{19,3},{20,4},{21,5},{22,6},{23,7},{24,8},{25... | collective-permute-start | bytes 2312 | tf_op jit(solution)/shard_map/ppermute | solution.py:18
  114.4 5.5 %collective-permute-start.20 = (bf16[48,1,258]{2,0,1:T(8,128)(2,1)S(1)}, bf16[48,1,258]{2,0,1:T(8,128)(2,1)S(1)}, u32[]{:S(2)}, u32[]{:S(2)}) collective-permute-start(bf16[48,1,258]{2,0,1:T(8,128)(2,1)S(1)} %get-tuple-element.18), channel_id=1, source_target_pairs={{0,1},{1,2},{2,3},{3,4},{4,5},{5,6},{6,7},{7,8},{8,9},{9,10},{10,1... | collective-permute-start | bytes 74312 | tf_op jit(solution)/shard_map/ppermute | solution.py:17
  117.7 6.2 %collective-permute-start.21 = (bf16[48,1,258]{2,0,1:T(8,128)(2,1)S(1)}, bf16[48,1,258]{2,0,1:T(8,128)(2,1)S(1)}, u32[]{:S(2)}, u32[]{:S(2)}) collective-permute-start(bf16[48,1,258]{2,0,1:T(8,128)(2,1)S(1)} %get-tuple-element.19), channel_id=1, source_target_pairs={{1,0},{2,1},{3,2},{4,3},{5,4},{6,5},{7,6},{8,7},{9,8},{10,9},{11,1... | collective-permute-start | bytes 74312 | tf_op jit(solution)/shard_map/ppermute | solution.py:18
  126.1 2.9 %collective-permute-start.22 = (bf16[48,8,1]{2,0,1:T(8,128)(2,1)S(1)}, bf16[48,8,1]{2,0,1:T(8,128)(2,1)S(1)}, u32[]{:S(2)}, u32[]{:S(2)}) collective-permute-start(bf16[48,8,1]{2,0,1:T(8,128)(2,1)S(1)} %get-tuple-element.38), channel_id=1, source_target_pairs={{0,16},{1,17},{2,18},{3,19},{4,20},{5,21},{6,22},{7,23},{8,24},{9,... | collective-permute-start | bytes 2312 | tf_op jit(solution)/shard_map/ppermute | solution.py:17
  127.4 5.4 %collective-permute-start.23 = (bf16[48,8,1]{2,0,1:T(8,128)(2,1)S(1)}, bf16[48,8,1]{2,0,1:T(8,128)(2,1)S(1)}, u32[]{:S(2)}, u32[]{:S(2)}) collective-permute-start(bf16[48,8,1]{2,0,1:T(8,128)(2,1)S(1)} %get-tuple-element.39), channel_id=1, source_target_pairs={{16,0},{17,1},{18,2},{19,3},{20,4},{21,5},{22,6},{23,7},{24,8},{25... | collective-permute-start | bytes 2312 | tf_op jit(solution)/shard_map/ppermute | solution.py:18
  132.8 5.5 %collective-permute-start.24 = (bf16[48,1,258]{2,0,1:T(8,128)(2,1)S(1)}, bf16[48,1,258]{2,0,1:T(8,128)(2,1)S(1)}, u32[]{:S(2)}, u32[]{:S(2)}) collective-permute-start(bf16[48,1,258]{2,0,1:T(8,128)(2,1)S(1)} %get-tuple-element.14), channel_id=1, source_target_pairs={{0,1},{1,2},{2,3},{3,4},{4,5},{5,6},{6,7},{7,8},{8,9},{9,10},{10,1... | collective-permute-start | bytes 74312 | tf_op jit(solution)/shard_map/ppermute | solution.py:17
  136.1 6.2 %collective-permute-start.25 = (bf16[48,1,258]{2,0,1:T(8,128)(2,1)S(1)}, bf16[48,1,258]{2,0,1:T(8,128)(2,1)S(1)}, u32[]{:S(2)}, u32[]{:S(2)}) collective-permute-start(bf16[48,1,258]{2,0,1:T(8,128)(2,1)S(1)} %get-tuple-element.15), channel_id=1, source_target_pairs={{1,0},{2,1},{3,2},{4,3},{5,4},{6,5},{7,6},{8,7},{9,8},{10,9},{11,1... | collective-permute-start | bytes 74312 | tf_op jit(solution)/shard_map/ppermute | solution.py:18
where the time goes:
time: 146 us; the launch traced here: 145 us
  starting transfers between devices  63.9 us (44%)
  waiting for transfers between devices  51.1 us (35%)
  matrix products  13.4 us (9%)
  local copies, waits for them, and re-layouts  6.89 us (5%)
  blocking collectives  6.17 us (4%)
  other arithmetic  3.07 us (2%)
    ppermute x13, waiting for transfers between devices, extended(): after = lax.ppermute(leading, axis, down)  45.7 us
    ppermute x13, starting transfers between devices, extended(): before = lax.ppermute(last, axis, up)  38.3 us
    ppermute x13, starting transfers between devices, extended(): after = lax.ppermute(leading, axis, down)  22.2 us
    dot_general x54, matrix products, conv_tile(): jnp.einsum('oi,ixy->oxy', kernel[a, b], padded[:, a:a + out_cols, b:b + o...  13.4 us
    psum x1, blocking collectives, shards(): ratio_sum = lax.psum(ratio_part, 'tm')  6.17 us
    all_to_all x1, starting transfers between devices, shards(): lax.all_to_all(features_own, 'tm', split_axis=2, concat_axis=0, tiled=True)  3.38 us
    all_to_all x1, waiting for transfers between devices, shards(): lax.all_to_all(features_own, 'tm', split_axis=2, concat_axis=0, tiled=True)  3.25 us
  transfers between devices with their start and end apart: 27, of which 19 were waited for; matrix products, arithmetic and copies ran while one was open for 2% of the time, Pallas kernels for 0%

commit v1 on v0

--- a/solution.py
+++ b/solution.py
@@ -44,6 +44,16 @@
 
 
 def shards(intensity, w_first, w_rest):
+
+    def _refer_trees(z_in, ax_name):
+        response = jnp.concatenate(
+            lax.all_to_all(
+                jnp.stack(jnp.split(z_in, lax.axis_size(ax_name), axis=2), axis=0), ax_name, 0, 0
+            ),
+            axis=0,
+        )
+        return response
+
     acq_dev, col_span, row_span = intensity.shape
     space_count = lax.axis_size("space")
     tm_count = lax.axis_size("tm")
@@ -66,7 +76,7 @@
     acq_total = acq_dev * tm_count
     ratio_sum = lax.psum(ratio_part, "tm")
     features_own = (log_mean + jnp.log(ratio_sum / acq_total)[None]).astype(jnp.bfloat16)
-    features = lax.all_to_all(features_own, "tm", split_axis=2, concat_axis=0, tiled=True)
+    features = _refer_trees(features_own, "tm")
     kernels = [w_first] + [w_rest[k] for k in range(LAYERS - 1)]
     activation = features
     result = None

time: 146 us -> 144 us (0.986)
  local copies, waits for them, and re-layouts: 6.89 us -> 2.87 us
    unnamed x11 -> x7, local copies, waits for them, and re-layouts: 2.53 us -> 0.03 us
  transfers between devices with their start and end apart: 27 -> 27, of which waited for: 19 -> 20; matrix products, arithmetic and copies ran while one was open for 2% -> 2% of each run, Pallas kernels for 0% -> 0%
where the time goes in v1:
time: 144 us; the launch traced here: 143 us
  starting transfers between devices  64.2 us (45%)
  waiting for transfers between devices  51.5 us (36%)
  matrix products  13.4 us (9%)
  blocking collectives  6.17 us (4%)
  other arithmetic  3.73 us (3%)
  local copies, waits for them, and re-layouts  2.87 us (2%)
    ppermute x13, waiting for transfers between devices, extended(): after = lax.ppermute(leading, axis, down)  46.4 us
    ppermute x13, starting transfers between devices, extended(): before = lax.ppermute(last, axis, up)  39 us
    ppermute x13, starting transfers between devices, extended(): after = lax.ppermute(leading, axis, down)  21.9 us
    dot_general x54, matrix products, conv_tile(): jnp.einsum('oi,ixy->oxy', kernel[a, b], padded[:, a:a + out_cols, b:b + o...  13.4 us
    psum x1, blocking collectives, shards(): ratio_sum = lax.psum(ratio_part, 'tm')  6.17 us
    all_to_all x1, starting transfers between devices, _refer_trees(): lax.all_to_all(jnp.stack(jnp.split(z_in, lax.axis_size(ax_name), axis=2),...  3.38 us
    all_to_all x1, waiting for transfers between devices, _refer_trees(): lax.all_to_all(jnp.stack(jnp.split(z_in, lax.axis_size(ax_name), axis=2),...  3.25 us
  transfers between devices with their start and end apart: 27, of which 20 were waited for; matrix products, arithmetic and copies ran while one was open for 2% of the time, Pallas kernels for 0%

profile of v1, /device:TPU:19, one launch (start us, length us, event | category | flops | bytes accessed | tf_op | source)
XLA Modules:
  0.0 142.7 jit_solution(14691894582306795041)
XLA Ops:
  0.0 1.1 fusion.193
  1.2 2.6 %collective-permute-start.1 = (f32[16,3,512]{2,1,0:T(4,128)S(1)}, f32[16,3,512]{2,1,0:T(4,128)S(1)}, u32[]{:S(2)}, u32[]{:S(2)}) collective-permute-start(f32[16,3,512]{2,1,0:T(4,128)S(1)} %get-tuple-element.36), channel_id=1, source_target_pairs={{1,0},{2,1},{3,2},{4,3},{5,4},{6,5},{7,6},{8,7},{9,8},{10,9},{11,1... | collective-permute-start | bytes 294920 | tf_op jit(solution)/shard_map/ppermute | solution.py:18
  3.7 3.9 %collective-permute-start = (f32[16,3,512]{2,1,0:T(4,128)S(1)}, f32[16,3,512]{2,1,0:T(4,128)S(1)}, u32[]{:S(2)}, u32[]{:S(2)}) collective-permute-start(f32[16,3,512]{2,1,0:T(4,128)S(1)} %get-tuple-element.37), channel_id=1, source_target_pairs={{0,1},{1,2},{2,3},{3,4},{4,5},{5,6},{6,7},{7,8},{8,9},{9,10},{10,1... | collective-permute-start | bytes 294920 | tf_op jit(solution)/shard_map/ppermute | solution.py:17
  7.8 0.6 collective-permute-done.1
  8.4 1.1 collective-permute-done
  9.8 0.5 fusion.66
  10.3 6.2 %psum.7 = f32[8,512]{1,0:T(8,128)S(1)} all-reduce(f32[8,512]{1,0:T(8,128)S(1)} %get-tuple-element.5), channel_id=1, replica_groups=mesh['tm'=2,'space'=16] {'tm'}, use_global_device_ids=true, to_apply=%region_1.2 | all-reduce | flops 4096 | bytes 32768 | tf_op jit(solution)/shard_map/psum | solution.py:77
  16.5 0.7 pad_maximum_fusion.31
  17.2 3.4 %all-to-all-start = ((bf16[2,16,8,256]{3,2,1,0:T(8,128)(2,1)}), bf16[2,16,8,256]{3,2,1,0:T(8,128)(2,1)S(1)}, u32[]{:S(2)}, u32[]{:S(2)}) async-start(bf16[2,16,8,256]{3,2,1,0:T(8,128)(2,1)} %pad_maximum_fusion.31), calls=%async_computation | async-start | bytes 262144 | tf_op jit(solution)/shard_map/all_to_all | solution.py:50
  20.7 3.3 %all-to-all-done = bf16[2,16,8,256]{3,2,1,0:T(8,128)(2,1)S(1)} async-done(((bf16[2,16,8,256]{3,2,1,0:T(8,128)(2,1)}), bf16[2,16,8,256]{3,2,1,0:T(8,128)(2,1)S(1)}, u32[]{:S(2)}, u32[]{:S(2)}) %all-to-all-start) | async-done | bytes 131104 | tf_op jit(solution)/shard_map/all_to_all | solution.py:50
  24.0 1.9 %collective-permute-start.2 = (bf16[32,8,1]{2,0,1:T(8,128)(2,1)S(1)}, bf16[32,8,1]{2,0,1:T(8,128)(2,1)S(1)}, u32[]{:S(2)}, u32[]{:S(2)}) collective-permute-start(bf16[32,8,1]{2,0,1:T(8,128)(2,1)S(1)} %get-tuple-element.48), channel_id=1, source_target_pairs={{0,16},{1,17},{2,18},{3,19},{4,20},{5,21},{6,22},{7,23},{8,24},{9,... | collective-permute-start | bytes 1544 | tf_op jit(solution)/shard_map/ppermute | solution.py:17
  26.0 1.3 collective-permute-start.3
  27.5 3.4 %collective-permute-done.3 = bf16[32,8,1]{2,0,1:T(8,128)(2,1)S(1)} collective-permute-done((bf16[32,8,1]{2,0,1:T(8,128)(2,1)S(1)}, bf16[32,8,1]{2,0,1:T(8,128)(2,1)S(1)}, u32[]{:S(2)}, u32[]{:S(2)}) %collective-permute-start.3) | collective-permute-done | bytes 544 | tf_op jit(solution)/shard_map/ppermute | solution.py:18
  31.1 10.2 %collective-permute-start.4 = (bf16[32,1,258]{2,0,1:T(8,128)(2,1)S(1)}, bf16[32,1,258]{2,0,1:T(8,128)(2,1)S(1)}, u32[]{:S(2)}, u32[]{:S(2)}) collective-permute-start(bf16[32,1,258]{2,0,1:T(8,128)(2,1)S(1)} %get-tuple-element.34), channel_id=1, source_target_pairs={{0,1},{1,2},{2,3},{3,4},{4,5},{5,6},{6,7},{7,8},{8,9},{9,10},{10,1... | collective-permute-start | bytes 49544 | tf_op jit(solution)/shard_map/ppermute | solution.py:17
  41.2 1.9 %collective-permute-start.5 = (bf16[32,1,258]{2,0,1:T(8,128)(2,1)S(1)}, bf16[32,1,258]{2,0,1:T(8,128)(2,1)S(1)}, u32[]{:S(2)}, u32[]{:S(2)}) collective-permute-start(bf16[32,1,258]{2,0,1:T(8,128)(2,1)S(1)} %get-tuple-element.35), channel_id=1, source_target_pairs={{1,0},{2,1},{3,2},{4,3},{5,4},{6,5},{7,6},{8,7},{9,8},{10,9},{11,1... | collective-permute-start | bytes 49544 | tf_op jit(solution)/shard_map/ppermute | solution.py:18
  43.2 0.3 fusion.144
  43.5 3.8 %collective-permute-done.5 = bf16[32,1,258]{2,0,1:T(8,128)(2,1)S(1)} collective-permute-done((bf16[32,1,258]{2,0,1:T(8,128)(2,1)S(1)}, bf16[32,1,258]{2,0,1:T(8,128)(2,1)S(1)}, u32[]{:S(2)}, u32[]{:S(2)}) %collective-permute-start.5) | collective-permute-done | bytes 16544 | tf_op jit(solution)/shard_map/ppermute | solution.py:18
  47.5 0.3 fusion.146
  47.8 0.3 fusion.148
  48.1 0.3 fusion.137
  48.4 0.3 fusion.139
  48.9 0.3 fusion.41
  49.2 0.3 fusion.51
  49.6 1.3 collective-permute-start.6
  50.9 1.3 collective-permute-start.7
  52.5 3.7 %collective-permute-done.7 = bf16[48,8,1]{2,0,1:T(8,128)(2,1)S(1)} collective-permute-done((bf16[48,8,1]{2,0,1:T(8,128)(2,1)S(1)}, bf16[48,8,1]{2,0,1:T(8,128)(2,1)S(1)}, u32[]{:S(2)}, u32[]{:S(2)}) %collective-permute-start.7) | collective-permute-done | bytes 800 | tf_op jit(solution)/shard_map/ppermute | solution.py:18
  56.4 3.4 %collective-permute-start.8 = (bf16[48,1,258]{2,0,1:T(8,128)(2,1)S(1)}, bf16[48,1,258]{2,0,1:T(8,128)(2,1)S(1)}, u32[]{:S(2)}, u32[]{:S(2)}) collective-permute-start(bf16[48,1,258]{2,0,1:T(8,128)(2,1)S(1)} %get-tuple-element.30), channel_id=1, source_target_pairs={{0,1},{1,2},{2,3},{3,4},{4,5},{5,6},{6,7},{7,8},{8,9},{9,10},{10,1... | collective-permute-start | bytes 74312 | tf_op jit(solution)/shard_map/ppermute | solution.py:17
  59.7 1.9 %collective-permute-start.9 = (bf16[48,1,258]{2,0,1:T(8,128)(2,1)S(1)}, bf16[48,1,258]{2,0,1:T(8,128)(2,1)S(1)}, u32[]{:S(2)}, u32[]{:S(2)}) collective-permute-start(bf16[48,1,258]{2,0,1:T(8,128)(2,1)S(1)} %get-tuple-element.31), channel_id=1, source_target_pairs={{1,0},{2,1},{3,2},{4,3},{5,4},{6,5},{7,6},{8,7},{9,8},{10,9},{11,1... | collective-permute-start | bytes 74312 | tf_op jit(solution)/shard_map/ppermute | solution.py:18
  62.0 4.0 %collective-permute-done.9 = bf16[48,1,258]{2,0,1:T(8,128)(2,1)S(1)} collective-permute-done((bf16[48,1,258]{2,0,1:T(8,128)(2,1)S(1)}, bf16[48,1,258]{2,0,1:T(8,128)(2,1)S(1)}, u32[]{:S(2)}, u32[]{:S(2)}) %collective-permute-start.9) | collective-permute-done | bytes 24800 | tf_op jit(solution)/shard_map/ppermute | solution.py:18
  65.9 0.3 maximum_maximum_fusion
  67.7 0.3 fusion.50
  68.1 1.3 collective-permute-start.10
  69.4 1.3 collective-permute-start.11
  71.0 3.7 %collective-permute-done.11 = bf16[48,8,1]{2,0,1:T(8,128)(2,1)S(1)} collective-permute-done((bf16[48,8,1]{2,0,1:T(8,128)(2,1)S(1)}, bf16[48,8,1]{2,0,1:T(8,128)(2,1)S(1)}, u32[]{:S(2)}, u32[]{:S(2)}) %collective-permute-start.11) | collective-permute-done | bytes 800 | tf_op jit(solution)/shard_map/ppermute | solution.py:18
  74.9 3.3 %collective-permute-start.12 = (bf16[48,1,258]{2,0,1:T(8,128)(2,1)S(1)}, bf16[48,1,258]{2,0,1:T(8,128)(2,1)S(1)}, u32[]{:S(2)}, u32[]{:S(2)}) collective-permute-start(bf16[48,1,258]{2,0,1:T(8,128)(2,1)S(1)} %get-tuple-element.26), channel_id=1, source_target_pairs={{0,1},{1,2},{2,3},{3,4},{4,5},{5,6},{6,7},{7,8},{8,9},{9,10},{10,1... | collective-permute-start | bytes 74312 | tf_op jit(solution)/shard_map/ppermute | solution.py:17
  78.2 1.9 %collective-permute-start.13 = (bf16[48,1,258]{2,0,1:T(8,128)(2,1)S(1)}, bf16[48,1,258]{2,0,1:T(8,128)(2,1)S(1)}, u32[]{:S(2)}, u32[]{:S(2)}) collective-permute-start(bf16[48,1,258]{2,0,1:T(8,128)(2,1)S(1)} %get-tuple-element.27), channel_id=1, source_target_pairs={{1,0},{2,1},{3,2},{4,3},{5,4},{6,5},{7,6},{8,7},{9,8},{10,9},{11,1... | collective-permute-start | bytes 74312 | tf_op jit(solution)/shard_map/ppermute | solution.py:18
  80.4 4.0 %collective-permute-done.13 = bf16[48,1,258]{2,0,1:T(8,128)(2,1)S(1)} collective-permute-done((bf16[48,1,258]{2,0,1:T(8,128)(2,1)S(1)}, bf16[48,1,258]{2,0,1:T(8,128)(2,1)S(1)}, u32[]{:S(2)}, u32[]{:S(2)}) %collective-permute-start.13) | collective-permute-done | bytes 24800 | tf_op jit(solution)/shard_map/ppermute | solution.py:18
  84.4 0.3 maximum_maximum_fusion.1
  86.1 0.3 fusion.49
  86.6 1.3 collective-permute-start.14
  87.9 1.3 collective-permute-start.15
  89.5 3.7 %collective-permute-done.15 = bf16[48,8,1]{2,0,1:T(8,128)(2,1)S(1)} collective-permute-done((bf16[48,8,1]{2,0,1:T(8,128)(2,1)S(1)}, bf16[48,8,1]{2,0,1:T(8,128)(2,1)S(1)}, u32[]{:S(2)}, u32[]{:S(2)}) %collective-permute-start.15) | collective-permute-done | bytes 800 | tf_op jit(solution)/shard_map/ppermute | solution.py:18
  93.3 3.3 %collective-permute-start.16 = (bf16[48,1,258]{2,0,1:T(8,128)(2,1)S(1)}, bf16[48,1,258]{2,0,1:T(8,128)(2,1)S(1)}, u32[]{:S(2)}, u32[]{:S(2)}) collective-permute-start(bf16[48,1,258]{2,0,1:T(8,128)(2,1)S(1)} %get-tuple-element.22), channel_id=1, source_target_pairs={{0,1},{1,2},{2,3},{3,4},{4,5},{5,6},{6,7},{7,8},{8,9},{9,10},{10,1... | collective-permute-start | bytes 74312 | tf_op jit(solution)/shard_map/ppermute | solution.py:17
  96.6 1.9 %collective-permute-start.17 = (bf16[48,1,258]{2,0,1:T(8,128)(2,1)S(1)}, bf16[48,1,258]{2,0,1:T(8,128)(2,1)S(1)}, u32[]{:S(2)}, u32[]{:S(2)}) collective-permute-start(bf16[48,1,258]{2,0,1:T(8,128)(2,1)S(1)} %get-tuple-element.23), channel_id=1, source_target_pairs={{1,0},{2,1},{3,2},{4,3},{5,4},{6,5},{7,6},{8,7},{9,8},{10,9},{11,1... | collective-permute-start | bytes 74312 | tf_op jit(solution)/shard_map/ppermute | solution.py:18
  98.8 4.0 %collective-permute-done.17 = bf16[48,1,258]{2,0,1:T(8,128)(2,1)S(1)} collective-permute-done((bf16[48,1,258]{2,0,1:T(8,128)(2,1)S(1)}, bf16[48,1,258]{2,0,1:T(8,128)(2,1)S(1)}, u32[]{:S(2)}, u32[]{:S(2)}) %collective-permute-start.17) | collective-permute-done | bytes 24800 | tf_op jit(solution)/shard_map/ppermute | solution.py:18
  102.8 0.3 maximum_maximum_fusion.2
  104.6 0.3 fusion.48
  105.0 1.3 collective-permute-start.18
  106.3 1.3 collective-permute-start.19
  107.9 3.7 %collective-permute-done.19 = bf16[48,8,1]{2,0,1:T(8,128)(2,1)S(1)} collective-permute-done((bf16[48,8,1]{2,0,1:T(8,128)(2,1)S(1)}, bf16[48,8,1]{2,0,1:T(8,128)(2,1)S(1)}, u32[]{:S(2)}, u32[]{:S(2)}) %collective-permute-start.19) | collective-permute-done | bytes 800 | tf_op jit(solution)/shard_map/ppermute | solution.py:18
  111.8 3.3 %collective-permute-start.20 = (bf16[48,1,258]{2,0,1:T(8,128)(2,1)S(1)}, bf16[48,1,258]{2,0,1:T(8,128)(2,1)S(1)}, u32[]{:S(2)}, u32[]{:S(2)}) collective-permute-start(bf16[48,1,258]{2,0,1:T(8,128)(2,1)S(1)} %get-tuple-element.18), channel_id=1, source_target_pairs={{0,1},{1,2},{2,3},{3,4},{4,5},{5,6},{6,7},{7,8},{8,9},{9,10},{10,1... | collective-permute-start | bytes 74312 | tf_op jit(solution)/shard_map/ppermute | solution.py:17
  115.1 1.9 %collective-permute-start.21 = (bf16[48,1,258]{2,0,1:T(8,128)(2,1)S(1)}, bf16[48,1,258]{2,0,1:T(8,128)(2,1)S(1)}, u32[]{:S(2)}, u32[]{:S(2)}) collective-permute-start(bf16[48,1,258]{2,0,1:T(8,128)(2,1)S(1)} %get-tuple-element.19), channel_id=1, source_target_pairs={{1,0},{2,1},{3,2},{4,3},{5,4},{6,5},{7,6},{8,7},{9,8},{10,9},{11,1... | collective-permute-start | bytes 74312 | tf_op jit(solution)/shard_map/ppermute | solution.py:18
  117.3 4.0 %collective-permute-done.21 = bf16[48,1,258]{2,0,1:T(8,128)(2,1)S(1)} collective-permute-done((bf16[48,1,258]{2,0,1:T(8,128)(2,1)S(1)}, bf16[48,1,258]{2,0,1:T(8,128)(2,1)S(1)}, u32[]{:S(2)}, u32[]{:S(2)}) %collective-permute-start.21) | collective-permute-done | bytes 24800 | tf_op jit(solution)/shard_map/ppermute | solution.py:18
  121.3 0.3 maximum_maximum_fusion.3
  123.0 0.3 fusion.47
  123.4 1.3 collective-permute-start.22
  124.7 1.3 collective-permute-start.23
  126.4 3.7 %collective-permute-done.23 = bf16[48,8,1]{2,0,1:T(8,128)(2,1)S(1)} collective-permute-done((bf16[48,8,1]{2,0,1:T(8,128)(2,1)S(1)}, bf16[48,8,1]{2,0,1:T(8,128)(2,1)S(1)}, u32[]{:S(2)}, u32[]{:S(2)}) %collective-permute-start.23) | collective-permute-done | bytes 800 | tf_op jit(solution)/shard_map/ppermute | solution.py:18
  130.2 3.3 %collective-permute-start.24 = (bf16[48,1,258]{2,0,1:T(8,128)(2,1)S(1)}, bf16[48,1,258]{2,0,1:T(8,128)(2,1)S(1)}, u32[]{:S(2)}, u32[]{:S(2)}) collective-permute-start(bf16[48,1,258]{2,0,1:T(8,128)(2,1)S(1)} %get-tuple-element.14), channel_id=1, source_target_pairs={{0,1},{1,2},{2,3},{3,4},{4,5},{5,6},{6,7},{7,8},{8,9},{9,10},{10,1... | collective-permute-start | bytes 74312 | tf_op jit(solution)/shard_map/ppermute | solution.py:17
  133.5 1.9 %collective-permute-start.25 = (bf16[48,1,258]{2,0,1:T(8,128)(2,1)S(1)}, bf16[48,1,258]{2,0,1:T(8,128)(2,1)S(1)}, u32[]{:S(2)}, u32[]{:S(2)}) collective-permute-start(bf16[48,1,258]{2,0,1:T(8,128)(2,1)S(1)} %get-tuple-element.15), channel_id=1, source_target_pairs={{1,0},{2,1},{3,2},{4,3},{5,4},{6,5},{7,6},{8,7},{9,8},{10,9},{11,1... | collective-permute-start | bytes 74312 | tf_op jit(solution)/shard_map/ppermute | solution.py:18
  135.7 4.0 %collective-permute-done.25 = bf16[48,1,258]{2,0,1:T(8,128)(2,1)S(1)} collective-permute-done((bf16[48,1,258]{2,0,1:T(8,128)(2,1)S(1)}, bf16[48,1,258]{2,0,1:T(8,128)(2,1)S(1)}, u32[]{:S(2)}, u32[]{:S(2)}) %collective-permute-start.25) | collective-permute-done | bytes 24800 | tf_op jit(solution)/shard_map/ppermute | solution.py:18
  139.7 0.3 maximum_maximum_fusion.4
  141.5 0.3 fusion.14
  141.8 1.0 copy.5
  (84 shorter events, 12.5 us)
Async XLA Ops:
  0.0 7.7 %copy-start = (f32[16,8,512]{2,1,0:T(8,128)S(1)}, f32[16,8,512]{2,1,0:T(8,128)}, u32[]{:S(2)}) copy-start(f32[16,8,512]{2,1,0:T(8,128)} %param.3) | copy-start | bytes 786436
  1.2 7.2 %collective-permute-start.1 = (f32[16,3,512]{2,1,0:T(4,128)S(1)}, f32[16,3,512]{2,1,0:T(4,128)S(1)}, u32[]{:S(2)}, u32[]{:S(2)}) collective-permute-start(f32[16,3,512]{2,1,0:T(4,128)S(1)} %get-tuple-element.36), channel_id=1, source_target_pairs={{1,0},{2,1},{3,2},{4,3},{5,4},{6,5},{7,6},{8,7},{9,8},{10,9},{11,1... | collective-permute-start | bytes 294920 | tf_op jit(solution)/shard_map/ppermute | solution.py:18
  3.7 5.8 %collective-permute-start = (f32[16,3,512]{2,1,0:T(4,128)S(1)}, f32[16,3,512]{2,1,0:T(4,128)S(1)}, u32[]{:S(2)}, u32[]{:S(2)}) collective-permute-start(f32[16,3,512]{2,1,0:T(4,128)S(1)} %get-tuple-element.37), channel_id=1, source_target_pairs={{0,1},{1,2},{2,3},{3,4},{4,5},{5,6},{6,7},{7,8},{8,9},{9,10},{10,1... | collective-permute-start | bytes 294920 | tf_op jit(solution)/shard_map/ppermute | solution.py:17
  16.4 4.2 %copy-start.1 = (bf16[5,3,3,48,48]{4,3,2,1,0:T(8,128)(2,1)S(1)}, bf16[5,3,3,48,48]{4,3,2,1,0:T(8,128)(2,1)}, u32[]{:S(2)}) copy-start(bf16[5,3,3,48,48]{4,3,2,1,0:T(8,128)(2,1)} %param.5) | copy-start | bytes 622084
  17.2 6.7 %all-to-all-start = ((bf16[2,16,8,256]{3,2,1,0:T(8,128)(2,1)}), bf16[2,16,8,256]{3,2,1,0:T(8,128)(2,1)S(1)}, u32[]{:S(2)}, u32[]{:S(2)}) async-start(bf16[2,16,8,256]{3,2,1,0:T(8,128)(2,1)} %pad_maximum_fusion.31), calls=%async_computation | async-start | bytes 262144 | tf_op jit(solution)/shard_map/all_to_all | solution.py:50
  23.9 3.3 %copy-start.2 = (bf16[3,3,48,32]{2,3,1,0:T(8,128)(2,1)S(1)}, bf16[3,3,48,32]{2,3,1,0:T(8,128)(2,1)}, u32[]{:S(2)}) copy-start(bf16[3,3,48,32]{2,3,1,0:T(8,128)(2,1)} %param.4) | copy-start | bytes 82948
  24.0 3.5 %collective-permute-start.2 = (bf16[32,8,1]{2,0,1:T(8,128)(2,1)S(1)}, bf16[32,8,1]{2,0,1:T(8,128)(2,1)S(1)}, u32[]{:S(2)}, u32[]{:S(2)}) collective-permute-start(bf16[32,8,1]{2,0,1:T(8,128)(2,1)S(1)} %get-tuple-element.48), channel_id=1, source_target_pairs={{0,16},{1,17},{2,18},{3,19},{4,20},{5,21},{6,22},{7,23},{8,24},{9,... | collective-permute-start | bytes 1544 | tf_op jit(solution)/shard_map/ppermute | solution.py:17
  26.0 5.0 %collective-permute-start.3 = (bf16[32,8,1]{2,0,1:T(8,128)(2,1)S(1)}, bf16[32,8,1]{2,0,1:T(8,128)(2,1)S(1)}, u32[]{:S(2)}, u32[]{:S(2)}) collective-permute-start(bf16[32,8,1]{2,0,1:T(8,128)(2,1)S(1)} %get-tuple-element.49), channel_id=1, source_target_pairs={{16,0},{17,1},{18,2},{19,3},{20,4},{21,5},{22,6},{23,7},{24,8},{25... | collective-permute-start | bytes 1544 | tf_op jit(solution)/shard_map/ppermute | solution.py:18
  31.1 12.4 %collective-permute-start.4 = (bf16[32,1,258]{2,0,1:T(8,128)(2,1)S(1)}, bf16[32,1,258]{2,0,1:T(8,128)(2,1)S(1)}, u32[]{:S(2)}, u32[]{:S(2)}) collective-permute-start(bf16[32,1,258]{2,0,1:T(8,128)(2,1)S(1)} %get-tuple-element.34), channel_id=1, source_target_pairs={{0,1},{1,2},{2,3},{3,4},{4,5},{5,6},{6,7},{7,8},{8,9},{9,10},{10,1... | collective-permute-start | bytes 49544 | tf_op jit(solution)/shard_map/ppermute | solution.py:17
  41.2 6.0 %collective-permute-start.5 = (bf16[32,1,258]{2,0,1:T(8,128)(2,1)S(1)}, bf16[32,1,258]{2,0,1:T(8,128)(2,1)S(1)}, u32[]{:S(2)}, u32[]{:S(2)}) collective-permute-start(bf16[32,1,258]{2,0,1:T(8,128)(2,1)S(1)} %get-tuple-element.35), channel_id=1, source_target_pairs={{1,0},{2,1},{3,2},{4,3},{5,4},{6,5},{7,6},{8,7},{9,8},{10,9},{11,1... | collective-permute-start | bytes 49544 | tf_op jit(solution)/shard_map/ppermute | solution.py:18
  49.6 2.9 %collective-permute-start.6 = (bf16[48,8,1]{2,0,1:T(8,128)(2,1)S(1)}, bf16[48,8,1]{2,0,1:T(8,128)(2,1)S(1)}, u32[]{:S(2)}, u32[]{:S(2)}) collective-permute-start(bf16[48,8,1]{2,0,1:T(8,128)(2,1)S(1)} %get-tuple-element.46), channel_id=1, source_target_pairs={{0,16},{1,17},{2,18},{3,19},{4,20},{5,21},{6,22},{7,23},{8,24},{9,... | collective-permute-start | bytes 2312 | tf_op jit(solution)/shard_map/ppermute | solution.py:17
  50.9 5.4 %collective-permute-start.7 = (bf16[48,8,1]{2,0,1:T(8,128)(2,1)S(1)}, bf16[48,8,1]{2,0,1:T(8,128)(2,1)S(1)}, u32[]{:S(2)}, u32[]{:S(2)}) collective-permute-start(bf16[48,8,1]{2,0,1:T(8,128)(2,1)S(1)} %get-tuple-element.47), channel_id=1, source_target_pairs={{16,0},{17,1},{18,2},{19,3},{20,4},{21,5},{22,6},{23,7},{24,8},{25... | collective-permute-start | bytes 2312 | tf_op jit(solution)/shard_map/ppermute | solution.py:18
  56.4 5.6 %collective-permute-start.8 = (bf16[48,1,258]{2,0,1:T(8,128)(2,1)S(1)}, bf16[48,1,258]{2,0,1:T(8,128)(2,1)S(1)}, u32[]{:S(2)}, u32[]{:S(2)}) collective-permute-start(bf16[48,1,258]{2,0,1:T(8,128)(2,1)S(1)} %get-tuple-element.30), channel_id=1, source_target_pairs={{0,1},{1,2},{2,3},{3,4},{4,5},{5,6},{6,7},{7,8},{8,9},{9,10},{10,1... | collective-permute-start | bytes 74312 | tf_op jit(solution)/shard_map/ppermute | solution.py:17
  59.7 6.2 %collective-permute-start.9 = (bf16[48,1,258]{2,0,1:T(8,128)(2,1)S(1)}, bf16[48,1,258]{2,0,1:T(8,128)(2,1)S(1)}, u32[]{:S(2)}, u32[]{:S(2)}) collective-permute-start(bf16[48,1,258]{2,0,1:T(8,128)(2,1)S(1)} %get-tuple-element.31), channel_id=1, source_target_pairs={{1,0},{2,1},{3,2},{4,3},{5,4},{6,5},{7,6},{8,7},{9,8},{10,9},{11,1... | collective-permute-start | bytes 74312 | tf_op jit(solution)/shard_map/ppermute | solution.py:18
  68.1 2.9 %collective-permute-start.10 = (bf16[48,8,1]{2,0,1:T(8,128)(2,1)S(1)}, bf16[48,8,1]{2,0,1:T(8,128)(2,1)S(1)}, u32[]{:S(2)}, u32[]{:S(2)}) collective-permute-start(bf16[48,8,1]{2,0,1:T(8,128)(2,1)S(1)} %get-tuple-element.44), channel_id=1, source_target_pairs={{0,16},{1,17},{2,18},{3,19},{4,20},{5,21},{6,22},{7,23},{8,24},{9,... | collective-permute-start | bytes 2312 | tf_op jit(solution)/shard_map/ppermute | solution.py:17
  69.4 5.4 %collective-permute-start.11 = (bf16[48,8,1]{2,0,1:T(8,128)(2,1)S(1)}, bf16[48,8,1]{2,0,1:T(8,128)(2,1)S(1)}, u32[]{:S(2)}, u32[]{:S(2)}) collective-permute-start(bf16[48,8,1]{2,0,1:T(8,128)(2,1)S(1)} %get-tuple-element.45), channel_id=1, source_target_pairs={{16,0},{17,1},{18,2},{19,3},{20,4},{21,5},{22,6},{23,7},{24,8},{25... | collective-permute-start | bytes 2312 | tf_op jit(solution)/shard_map/ppermute | solution.py:18
  74.9 5.5 %collective-permute-start.12 = (bf16[48,1,258]{2,0,1:T(8,128)(2,1)S(1)}, bf16[48,1,258]{2,0,1:T(8,128)(2,1)S(1)}, u32[]{:S(2)}, u32[]{:S(2)}) collective-permute-start(bf16[48,1,258]{2,0,1:T(8,128)(2,1)S(1)} %get-tuple-element.26), channel_id=1, source_target_pairs={{0,1},{1,2},{2,3},{3,4},{4,5},{5,6},{6,7},{7,8},{8,9},{9,10},{10,1... | collective-permute-start | bytes 74312 | tf_op jit(solution)/shard_map/ppermute | solution.py:17
  78.2 6.2 %collective-permute-start.13 = (bf16[48,1,258]{2,0,1:T(8,128)(2,1)S(1)}, bf16[48,1,258]{2,0,1:T(8,128)(2,1)S(1)}, u32[]{:S(2)}, u32[]{:S(2)}) collective-permute-start(bf16[48,1,258]{2,0,1:T(8,128)(2,1)S(1)} %get-tuple-element.27), channel_id=1, source_target_pairs={{1,0},{2,1},{3,2},{4,3},{5,4},{6,5},{7,6},{8,7},{9,8},{10,9},{11,1... | collective-permute-start | bytes 74312 | tf_op jit(solution)/shard_map/ppermute | solution.py:18
  86.6 2.9 %collective-permute-start.14 = (bf16[48,8,1]{2,0,1:T(8,128)(2,1)S(1)}, bf16[48,8,1]{2,0,1:T(8,128)(2,1)S(1)}, u32[]{:S(2)}, u32[]{:S(2)}) collective-permute-start(bf16[48,8,1]{2,0,1:T(8,128)(2,1)S(1)} %get-tuple-element.42), channel_id=1, source_target_pairs={{0,16},{1,17},{2,18},{3,19},{4,20},{5,21},{6,22},{7,23},{8,24},{9,... | collective-permute-start | bytes 2312 | tf_op jit(solution)/shard_map/ppermute | solution.py:17
  87.9 5.4 %collective-permute-start.15 = (bf16[48,8,1]{2,0,1:T(8,128)(2,1)S(1)}, bf16[48,8,1]{2,0,1:T(8,128)(2,1)S(1)}, u32[]{:S(2)}, u32[]{:S(2)}) collective-permute-start(bf16[48,8,1]{2,0,1:T(8,128)(2,1)S(1)} %get-tuple-element.43), channel_id=1, source_target_pairs={{16,0},{17,1},{18,2},{19,3},{20,4},{21,5},{22,6},{23,7},{24,8},{25... | collective-permute-start | bytes 2312 | tf_op jit(solution)/shard_map/ppermute | solution.py:18
  93.3 5.5 %collective-permute-start.16 = (bf16[48,1,258]{2,0,1:T(8,128)(2,1)S(1)}, bf16[48,1,258]{2,0,1:T(8,128)(2,1)S(1)}, u32[]{:S(2)}, u32[]{:S(2)}) collective-permute-start(bf16[48,1,258]{2,0,1:T(8,128)(2,1)S(1)} %get-tuple-element.22), channel_id=1, source_target_pairs={{0,1},{1,2},{2,3},{3,4},{4,5},{5,6},{6,7},{7,8},{8,9},{9,10},{10,1... | collective-permute-start | bytes 74312 | tf_op jit(solution)/shard_map/ppermute | solution.py:17
  96.6 6.2 %collective-permute-start.17 = (bf16[48,1,258]{2,0,1:T(8,128)(2,1)S(1)}, bf16[48,1,258]{2,0,1:T(8,128)(2,1)S(1)}, u32[]{:S(2)}, u32[]{:S(2)}) collective-permute-start(bf16[48,1,258]{2,0,1:T(8,128)(2,1)S(1)} %get-tuple-element.23), channel_id=1, source_target_pairs={{1,0},{2,1},{3,2},{4,3},{5,4},{6,5},{7,6},{8,7},{9,8},{10,9},{11,1... | collective-permute-start | bytes 74312 | tf_op jit(solution)/shard_map/ppermute | solution.py:18
  105.0 2.9 %collective-permute-start.18 = (bf16[48,8,1]{2,0,1:T(8,128)(2,1)S(1)}, bf16[48,8,1]{2,0,1:T(8,128)(2,1)S(1)}, u32[]{:S(2)}, u32[]{:S(2)}) collective-permute-start(bf16[48,8,1]{2,0,1:T(8,128)(2,1)S(1)} %get-tuple-element.40), channel_id=1, source_target_pairs={{0,16},{1,17},{2,18},{3,19},{4,20},{5,21},{6,22},{7,23},{8,24},{9,... | collective-permute-start | bytes 2312 | tf_op jit(solution)/shard_map/ppermute | solution.py:17
  106.3 5.4 %collective-permute-start.19 = (bf16[48,8,1]{2,0,1:T(8,128)(2,1)S(1)}, bf16[48,8,1]{2,0,1:T(8,128)(2,1)S(1)}, u32[]{:S(2)}, u32[]{:S(2)}) collective-permute-start(bf16[48,8,1]{2,0,1:T(8,128)(2,1)S(1)} %get-tuple-element.41), channel_id=1, source_target_pairs={{16,0},{17,1},{18,2},{19,3},{20,4},{21,5},{22,6},{23,7},{24,8},{25... | collective-permute-start | bytes 2312 | tf_op jit(solution)/shard_map/ppermute | solution.py:18
  111.8 5.5 %collective-permute-start.20 = (bf16[48,1,258]{2,0,1:T(8,128)(2,1)S(1)}, bf16[48,1,258]{2,0,1:T(8,128)(2,1)S(1)}, u32[]{:S(2)}, u32[]{:S(2)}) collective-permute-start(bf16[48,1,258]{2,0,1:T(8,128)(2,1)S(1)} %get-tuple-element.18), channel_id=1, source_target_pairs={{0,1},{1,2},{2,3},{3,4},{4,5},{5,6},{6,7},{7,8},{8,9},{9,10},{10,1... | collective-permute-start | bytes 74312 | tf_op jit(solution)/shard_map/ppermute | solution.py:17
  115.1 6.2 %collective-permute-start.21 = (bf16[48,1,258]{2,0,1:T(8,128)(2,1)S(1)}, bf16[48,1,258]{2,0,1:T(8,128)(2,1)S(1)}, u32[]{:S(2)}, u32[]{:S(2)}) collective-permute-start(bf16[48,1,258]{2,0,1:T(8,128)(2,1)S(1)} %get-tuple-element.19), channel_id=1, source_target_pairs={{1,0},{2,1},{3,2},{4,3},{5,4},{6,5},{7,6},{8,7},{9,8},{10,9},{11,1... | collective-permute-start | bytes 74312 | tf_op jit(solution)/shard_map/ppermute | solution.py:18
  123.4 2.9 %collective-permute-start.22 = (bf16[48,8,1]{2,0,1:T(8,128)(2,1)S(1)}, bf16[48,8,1]{2,0,1:T(8,128)(2,1)S(1)}, u32[]{:S(2)}, u32[]{:S(2)}) collective-permute-start(bf16[48,8,1]{2,0,1:T(8,128)(2,1)S(1)} %get-tuple-element.38), channel_id=1, source_target_pairs={{0,16},{1,17},{2,18},{3,19},{4,20},{5,21},{6,22},{7,23},{8,24},{9,... | collective-permute-start | bytes 2312 | tf_op jit(solution)/shard_map/ppermute | solution.py:17
  124.7 5.4 %collective-permute-start.23 = (bf16[48,8,1]{2,0,1:T(8,128)(2,1)S(1)}, bf16[48,8,1]{2,0,1:T(8,128)(2,1)S(1)}, u32[]{:S(2)}, u32[]{:S(2)}) collective-permute-start(bf16[48,8,1]{2,0,1:T(8,128)(2,1)S(1)} %get-tuple-element.39), channel_id=1, source_target_pairs={{16,0},{17,1},{18,2},{19,3},{20,4},{21,5},{22,6},{23,7},{24,8},{25... | collective-permute-start | bytes 2312 | tf_op jit(solution)/shard_map/ppermute | solution.py:18
  130.2 5.5 %collective-permute-start.24 = (bf16[48,1,258]{2,0,1:T(8,128)(2,1)S(1)}, bf16[48,1,258]{2,0,1:T(8,128)(2,1)S(1)}, u32[]{:S(2)}, u32[]{:S(2)}) collective-permute-start(bf16[48,1,258]{2,0,1:T(8,128)(2,1)S(1)} %get-tuple-element.14), channel_id=1, source_target_pairs={{0,1},{1,2},{2,3},{3,4},{4,5},{5,6},{6,7},{7,8},{8,9},{9,10},{10,1... | collective-permute-start | bytes 74312 | tf_op jit(solution)/shard_map/ppermute | solution.py:17
  133.5 6.2 %collective-permute-start.25 = (bf16[48,1,258]{2,0,1:T(8,128)(2,1)S(1)}, bf16[48,1,258]{2,0,1:T(8,128)(2,1)S(1)}, u32[]{:S(2)}, u32[]{:S(2)}) collective-permute-start(bf16[48,1,258]{2,0,1:T(8,128)(2,1)S(1)} %get-tuple-element.15), channel_id=1, source_target_pairs={{1,0},{2,1},{3,2},{4,3},{5,4},{6,5},{7,6},{8,7},{9,8},{10,9},{11,1... | collective-permute-start | bytes 74312 | tf_op jit(solution)/shard_map/ppermute | solution.py:18
